TPU v7x, 32 devices: a whole 2x2x4 slice. The times are simulated.
32 devices in a mesh: rep: 4 (over x, core), ep: 4 (over z), grp: 2 (over y).
Axes of the slice: x: 2, y: 2, z: 4, core: 2. Of those that a mesh axis runs over, the one named last changes fastest.
Arguments:
- tokens: bfloat16 [4096, 2048], P(('rep', 'ep', 'grp')), may hold values from -6 to 6
- grad_out: bfloat16 [4096, 2048], P(('rep', 'ep', 'grp')), may hold values from -6 to 6
- expert_ids: int32 [4096, 2], P(('rep', 'ep', 'grp')), may hold values from 0 to 7, as said below
- combine: bfloat16 [4096, 2], P(('rep', 'ep', 'grp')), may hold values from 0.099609375 to 1
- weights: bfloat16 [2048, 3, 7168], P('grp', None, 'ep'), may hold values from -0.125 to 0.125
Outputs:
- grad_tokens: bfloat16 [4096, 2048], P(('rep', 'ep', 'grp'))
- grad_combine: float32 [4096, 2], P(('rep', 'ep', 'grp'))
- grad_weights: float32 [2048, 3, 7168], P(('rep', 'grp'), None, 'ep')
Inputs may be any that keep to these rules, and one draw needn't show every extreme that they name: `expert_ids`: each token names 2 different experts, at most one of them below 1. No expert below 1 is named by more than 4 tokens of one device, and each of them is named by exactly 4 tokens of some device.
All inputs are finite; a program needn't handle non-finite values.
Results may differ from a plain program's by a relative error of at most 0.0085.
Values may be sent and summed in bfloat16 or wider, within the bound.
A program may use at most 128 MiB of HBM per device.

v0:
```python
import jax
import jax.numpy as jnp
from jax import lax
from jax.sharding import PartitionSpec as P

FLIGHT = 1
CAP = 4


def route_slots(routing, gate_vals):
    match = (routing == 0).astype(jnp.float32)
    assigned = jnp.sum(match, axis=1)
    combined = jnp.sum(match * gate_vals.astype(jnp.float32), axis=1)
    before = jnp.cumsum(assigned) - assigned
    slot_index = jnp.arange(CAP, dtype=jnp.float32)
    slot_map = (before[None, :] == slot_index[:, None]).astype(jnp.float32) * assigned[None, :]
    return (match, combined, slot_map)


def local(tokens, grad_out, expert_ids, combine, weights):
    ep, rep, grp = (lax.axis_size("ep"), lax.axis_size("rep"), lax.axis_size("grp"))
    me_g = lax.axis_index("grp")
    width = tokens.shape[1]
    half = width // grp
    owner = width // (rep * grp)
    hid = weights.shape[2]
    peers = ep * grp
    rows = peers * CAP
    pad = 128
    f32, bf16 = (jnp.float32, jnp.bfloat16)
    match, combined, slot_map = route_slots(expert_ids, combine)
    slot_bf = slot_map.astype(bf16)
    xs = jnp.dot(slot_bf, tokens, preferred_element_type=f32).astype(bf16)
    ys = jnp.dot(slot_bf, grad_out, preferred_element_type=f32).astype(bf16)
    cs = jnp.sum(slot_map * combined[None, :], axis=1).astype(bf16)
    sent = jnp.concatenate([xs, ys, jnp.broadcast_to(cs[:, None], (CAP, pad))], axis=1)
    got = lax.all_gather(sent, ("grp", "ep"), axis=0, tiled=True)
    pair = got[:, : 2 * width].reshape(rows, 2, width)
    scale = got[:, 2 * width : 2 * width + 1].astype(f32)
    mine = lax.dynamic_slice_in_dim(pair, me_g * half, half, axis=2)
    blocks = pair.reshape(rows, 2, rep, grp, owner)
    blocks = lax.dynamic_index_in_dim(blocks, me_g, axis=3, keepdims=False)
    blocks = jnp.transpose(blocks, (2, 0, 1, 3)).reshape(rep, rows, 2 * owner)
    cols = lax.all_to_all(blocks, "rep", split_axis=0, concat_axis=0, tiled=True)
    cols = cols.reshape(rep * rows, 2, owner)
    w = jnp.transpose(weights, (1, 0, 2))
    pre = jnp.concatenate(
        [
            jnp.dot(mine[:, 0], w[0], preferred_element_type=f32),
            jnp.dot(mine[:, 0], w[1], preferred_element_type=f32),
            jnp.dot(mine[:, 1], w[2], preferred_element_type=f32),
        ],
        axis=1,
    )
    pre = lax.psum(pre, "grp")
    a, b, back = (pre[:, :hid], pre[:, hid : 2 * hid], pre[:, 2 * hid :])
    sig = jax.nn.sigmoid(a)
    act = a * sig
    h = act * b
    dh = scale * back
    da = (dh * b * sig * (1.0 + a * (1.0 - sig))).astype(bf16)
    db = (dh * act).astype(bf16)
    hc = (scale * h).astype(bf16)
    pc = jnp.sum(h * back, axis=1, keepdims=True).astype(bf16)
    hidden = lax.all_gather(jnp.concatenate([da, db, hc], axis=1), "rep", axis=0, tiled=True)
    dn = (((1,), (1,)), ((), ()))
    px = lax.dot_general(da, w[0], dn, preferred_element_type=f32)
    px = (px + lax.dot_general(db, w[1], dn, preferred_element_type=f32)).astype(bf16)
    out = jnp.concatenate([px, jnp.broadcast_to(pc, (rows, pad))], axis=1)
    ret = lax.all_to_all(out, ("grp", "ep"), split_axis=0, concat_axis=0, tiled=True)
    ret = ret.reshape(grp, ep, CAP, half + pad).astype(f32)
    summed = jnp.sum(ret, axis=1)
    summed_x = jnp.transpose(summed[:, :, :half], (1, 0, 2)).reshape(CAP, width)
    summed_c = summed[0, :, half]
    highest = lax.Precision.HIGHEST
    tn = (((0,), (0,)), ((), ()))
    grad_tokens = lax.dot_general(slot_map, summed_x, tn, precision=highest).astype(bf16)
    per_token = jnp.sum(slot_map * summed_c[:, None], axis=0)
    grad_combine = match * per_token[:, None]
    gw = [
        lax.dot_general(
            cols[:, i], hidden[:, k * hid : (k + 1) * hid], tn, preferred_element_type=f32
        )
        for k, i in ((0, 0), (1, 0), (2, 1))
    ]
    return (grad_tokens, grad_combine, jnp.stack(gw, axis=1))


def solution(mesh):
    split = P(("rep", "ep", "grp"), None)
    in_specs = (split, split, split, split, P("grp", None, "ep"))
    out_specs = (split, split, P(("rep", "grp"), None, "ep"))
    return jax.shard_map(local, mesh=mesh, in_specs=in_specs, out_specs=out_specs, check_vma=False)
```

profile of v0, /device:TPU:0, one launch (start us, length us, event | category | flops | bytes accessed | tf_op | source)
XLA Modules:
  0.0 131.9 jit_solution(17238979611261452542)
XLA Ops:
  7.2 0.7 convert_reduce_fusion.2
  8.0 0.1 copy.35
  8.1 0.2 reduce-window.8
  8.4 0.1 fusion.18
  8.5 0.2 convolution_convert_fusion.1
  8.7 1.2 convolution_convert_fusion.2
  10.0 32.9 %all-gather = bf16[8,4,4224]{2,1,0:T(4,128)(2,1)S(1)} all-gather(bf16[1,4,4224]{2,1,0:T(4,128)(2,1)S(1)} %maximum_bitcast_fusion), channel_id=1, replica_groups=mesh['rep'=4,'ep'=4,'grp'=2] {'grp','ep'}, dimensions={0}, use_global_device_ids=true | all-gather | bytes 304128 | tf_op jit(solution)/shard_map/all_gather | solution.py:37
  43.0 0.2 reshape.66
  43.2 0.3 constant_dynamic-slice_fusion
  43.5 2.7 %fusion.2 = f32[32,1792]{1,0:T(8,128)S(1)} fusion(bf16[3,1024,1792]{2,1,0:T(8,128)(2,1)} %bitcast.58, bf16[32,1,1024]{2,1,0:T(2,128)(2,1)S(1)} %get-tuple-element.9), kind=kOutput, calls=%fused_computation.6 | convolution fusion | flops 117440512 | bytes 3964928 | tf_op jit(solution)/shard_map/dot_general | solution.py:49
  46.3 2.7 %fusion.4 = f32[32,1792]{1,0:T(8,128)S(1)} fusion(bf16[3,1024,1792]{2,1,0:T(8,128)(2,1)} %bitcast.59, bf16[32,1,1024]{2,1,0:T(2,128)(2,1)S(1)} %get-tuple-element.9), kind=kOutput, calls=%fused_computation.8 | convolution fusion | flops 117440512 | bytes 3964928 | tf_op jit(solution)/shard_map/dot_general | solution.py:50
  49.0 2.8 %fusion = f32[32,1792]{1,0:T(8,128)S(1)} fusion(bf16[3,1024,1792]{2,1,0:T(8,128)(2,1)} %bitcast.60, bf16[32,1,1024]{2,1,0:T(2,128)(2,1)S(1)} %get-tuple-element.10), kind=kOutput, calls=%fused_computation.2 | convolution fusion | flops 117440512 | bytes 3964928 | tf_op jit(solution)/shard_map/dot_general | solution.py:51
  51.8 0.9 pad_maximum_fusion.1
  52.7 0.2 reshape_reshape.3
  53.0 33.3 %all-reduce.2.cloned.1.call-done = f32[32,5376]{1,0:T(8,128)} async-done(((f32[32,5376]{1,0:T(8,128)}), f32[32,5376]{1,0:T(8,128)}) %all-reduce.2.cloned.1.call-update) | async-done | bytes 688144 | tf_op jit(solution)/shard_map/psum | solution.py:55
  86.3 1.4 %multiply_convert_fusion = (bf16[32,1792]{1,0:T(8,128)(2,1)S(1)}, bf16[32,1792]{1,0:T(8,128)(2,1)S(1)}, bf16[32,1792]{1,0:T(8,128)(2,1)S(1)}, bf16[32]{0:T(256)(128)(2,1)S(1)}) fusion(f32[32]{0:T(128)S(1)} %convert_reduce_fusion.1, f32[32,5376]{1,0:T(8,128)} %all-reduce.2.cloned.1.call-done), kind=kLoop, calls=%fused_computation.22 | loop fusion | flops 1089504 | bytes 1032384 | tf_op jit(solution)/shard_map/convert_element_type | solution.py:63
  87.7 0.8 pad_maximum_fusion.2
  88.5 0.3 constant_dynamic-slice_fusion.1
  88.9 7.1 %all_to_all.14 = bf16[4,32,512]{2,1,0:T(8,128)(2,1)S(1)} all-to-all(bf16[4,32,512]{2,1,0:T(8,128)(2,1)S(1)} %bitcast.64), channel_id=1, replica_groups=mesh['rep'=4,'ep'=4,'grp'=2] {'rep'}, dimensions={0} | all-to-all | bytes 262144 | tf_op jit(solution)/shard_map/all_to_all | solution.py:44
  96.1 3.2 %fusion.1 = f32[32,1024]{1,0:T(8,128)S(1)} fusion(bf16[32,1792]{1,0:T(8,128)(2,1)S(1)} %get-tuple-element.7, bf16[3,1024,1792]{2,1,0:T(8,128)(2,1)} %bitcast.61), kind=kOutput, calls=%fused_computation.5 | convolution fusion | flops 117440512 | bytes 3915776 | tf_op jit(solution)/shard_map/dot_general | solution.py:67
  99.3 3.2 %fusion.6 = bf16[32,1024]{1,0:T(8,128)(2,1)S(1)} fusion(f32[32,1024]{1,0:T(8,128)S(1)} %fusion.1, bf16[32,1792]{1,0:T(8,128)(2,1)S(1)} %get-tuple-element.6, bf16[3,1024,1792]{2,1,0:T(8,128)(2,1)} %bitcast.62), kind=kOutput, calls=%fused_computation.16 | convolution fusion | flops 117506048 | bytes 3981312 | tf_op jit(solution)/shard_map/dot_general | solution.py:68
  102.7 0.7 all_to_all.9
  103.3 4.9 %all-to-all-start = ((bf16[8,4,1152]{2,1,0:T(4,128)(2,1)}), bf16[8,4,1152]{2,1,0:T(4,128)(2,1)S(1)}, u32[]{:S(2)}, u32[]{:S(2)}) async-start(bf16[8,4,1152]{2,1,0:T(4,128)(2,1)} %all_to_all.9), calls=%async_computation | async-start | bytes 147456 | tf_op jit(solution)/shard_map/all_to_all | solution.py:70
  108.2 0.2 fusion.32
  108.4 6.9 %all-to-all-done = bf16[8,4,1152]{2,1,0:T(4,128)(2,1)S(1)} async-done(((bf16[8,4,1152]{2,1,0:T(4,128)(2,1)}), bf16[8,4,1152]{2,1,0:T(4,128)(2,1)S(1)}, u32[]{:S(2)}, u32[]{:S(2)}) %all-to-all-start) | async-done | bytes 73760 | tf_op jit(solution)/shard_map/all_to_all | solution.py:70
  115.3 0.1 slice_reduce_fusion
  115.5 0.6 broadcast_select_fusion
  116.1 1.8 %convolution_convert_fusion = bf16[128,2048]{1,0:T(8,128)(2,1)} fusion(f32[4,2048]{1,0:T(4,128)S(1)} %bitcast.65, f32[128]{0:T(128)S(1)} %get-tuple-element.3, f32[128]{0:T(128)S(1)} %sub.10), kind=kOutput, calls=%fused_computation.12 | convolution fusion | flops 12846080 | bytes 558080 | tf_op jit(solution)/shard_map/dot_general | solution.py:77
  117.9 1.4 %convolution_bitcast_fusion.1 = f32[256,1,1792]{2,0,1:T(8,128)S(1)} fusion(bf16[128,5376]{1,0:T(8,128)(2,1)} %all-gather.3.cloned.1.call-done, bf16[128,1,256]{2,1,0:T(2,128)(2,1)S(1)} %get-tuple-element.11), kind=kOutput, calls=%fused_computation.10 | convolution fusion | flops 117440512 | bytes 2359296 | tf_op jit(solution)/shard_map/dot_general | solution.py:81
  119.4 1.4 %convolution_bitcast_fusion.2 = f32[256,1,1792]{2,0,1:T(8,128)S(1)} fusion(bf16[128,5376]{1,0:T(8,128)(2,1)} %all-gather.3.cloned.1.call-done, bf16[128,1,256]{2,1,0:T(2,128)(2,1)S(1)} %get-tuple-element.11), kind=kOutput, calls=%fused_computation.11 | convolution fusion | flops 117440512 | bytes 2359296 | tf_op jit(solution)/shard_map/dot_general | solution.py:81
  120.8 1.4 %convolution_bitcast_fusion = f32[256,1,1792]{2,0,1:T(8,128)S(1)} fusion(bf16[128,5376]{1,0:T(8,128)(2,1)} %all-gather.3.cloned.1.call-done, bf16[128,1,256]{2,1,0:T(2,128)(2,1)S(1)} %get-tuple-element.12), kind=kOutput, calls=%fused_computation.9 | convolution fusion | flops 117440512 | bytes 2359296 | tf_op jit(solution)/shard_map/dot_general | solution.py:81
  122.2 2.8 %pad_maximum_fusion = f32[256,3,1792]{2,0,1:T(8,128)} fusion(f32[256,1,1792]{2,0,1:T(8,128)S(1)} %convolution_bitcast_fusion, f32[256,1,1792]{2,0,1:T(8,128)S(1)} %convolution_bitcast_fusion.1, f32[256,1,1792]{2,0,1:T(8,128)S(1)} %convolution_bitcast_fusion.2), kind=kLoop, calls=%fused_computation | loop fusion | flops 2752512 | bytes 11010048 | tf_op jit(solution)/shard_map/stack | solution.py:86
  (24 shorter events, 0.9 us)
Async XLA Ops:
  7.2 1.3 %copy-start = (bf16[128,2048]{1,0:T(8,128)(2,1)S(1)}, bf16[128,2048]{1,0:T(8,128)(2,1)}, u32[]{:S(2)}) copy-start(bf16[128,2048]{1,0:T(8,128)(2,1)} %param.6) | copy-start | bytes 1572868
  7.2 79.1 %all-reduce.2.cloned.1.call-start = ((), (), s32[]{:S(2)}) async-start(), calls=%async_computation.2 | async-start | bytes 1376256 | tf_op jit(solution)/shard_map/psum | solution.py:55
  52.7 65.2 %all-gather.3.cloned.1.call-start = ((), (), s32[]{:S(2)}) async-start(), calls=%async_computation.3 | async-start | bytes 1720320 | tf_op jit(solution)/shard_map/all_gather | solution.py:65
  96.1 19.4 %copy-start.1 = (s32[128,2]{0,1:T(2,128)S(1)}, s32[128,2]{0,1:T(2,128)}, u32[]{:S(2)}) copy-start(s32[128,2]{0,1:T(2,128)} %param.7) | copy-start | bytes 3076
  103.3 11.9 %all-to-all-start = ((bf16[8,4,1152]{2,1,0:T(4,128)(2,1)}), bf16[8,4,1152]{2,1,0:T(4,128)(2,1)S(1)}, u32[]{:S(2)}, u32[]{:S(2)}) async-start(bf16[8,4,1152]{2,1,0:T(4,128)(2,1)} %all_to_all.9), calls=%async_computation | async-start | bytes 147456 | tf_op jit(solution)/shard_map/all_to_all | solution.py:70
Sparse Core Ops, SparseCore 0:
  52.8 33.4 all-reduce.1
  88.7 18.5 all-gather.2
where the time goes:
time: 133 us; the launch traced here: 132 us
  waiting for transfers between devices  40.2 us (30%)
  blocking collectives  40 us (30%)
  matrix products  22.3 us (17%)
  between operations  14.2 us (11%)
  other arithmetic  7.88 us (6%)
  starting transfers between devices  4.95 us (4%)
  local copies, waits for them, and re-layouts  2.39 us (2%)
    psum x1, waiting for transfers between devices, local(): pre = lax.psum(pre, 'grp')  33.3 us
    all_gather x1, blocking collectives, local(): got = lax.all_gather(sent, ('grp', 'ep'), axis=0, tiled=True)  32.9 us
    all_to_all x1, blocking collectives, local(): lax.all_to_all(blocks, 'rep', split_axis=0, concat_axis=0, tiled=True)  7.14 us
    all_to_all x1, waiting for transfers between devices, local(): lax.all_to_all(out, ('grp', 'ep'), split_axis=0, concat_axis=0, tiled=True)  6.87 us
    all_to_all x1, starting transfers between devices, local(): lax.all_to_all(out, ('grp', 'ep'), split_axis=0, concat_axis=0, tiled=True)  4.87 us
    dot_general x3, matrix products, local(): lax.dot_general(cols[:, i], hidden[:, k * hid:(k + 1) * hid], tn, preferr...  4.31 us
    dot_general x1, matrix products, local(): lax.dot_general(db, w[1], dn, preferred_element_type=f32)  3.24 us
    dot_general x1, matrix products, local(): px = lax.dot_general(da, w[0], dn, preferred_element_type=f32)  3.21 us
  transfers between devices with their start and end apart: 3, of which 2 were waited for; matrix products, arithmetic and copies ran while one was open for 8% of the time, Pallas kernels for 0%

commit v1 on v0

--- a/solution.py
+++ b/solution.py
@@ -52,7 +52,7 @@
         ],
         axis=1,
     )
-    pre = lax.psum(pre, "grp")
+    pre = jnp.sum(lax.all_gather(pre, "grp"), axis=0)
     a, b, back = (pre[:, :hid], pre[:, hid : 2 * hid], pre[:, 2 * hid :])
     sig = jax.nn.sigmoid(a)
     act = a * sig

time: 133 us -> 126 us (0.947)
  waiting for transfers between devices: 40.2 us -> 32.9 us
    psum x1 -> x0, waiting for transfers between devices: 33.3 us -> none  [local(): pre = lax.psum(pre, 'grp')]
    all_gather x0 -> x1, waiting for transfers between devices: none -> 26 us  [local(): pre = jnp.sum(lax.all_gather(pre, 'grp'), axis=0)]
    reduce_sum x0 -> x1, other arithmetic: none -> 1.49 us  [local(): pre = jnp.sum(lax.all_gather(pre, 'grp'), axis=0)]
where the time goes in v1:
time: 126 us; the launch traced here: 125 us
  blocking collectives  40 us (32%)
  waiting for transfers between devices  32.9 us (26%)
  matrix products  22.3 us (18%)
  between operations  14.2 us (11%)
  other arithmetic  8.16 us (6%)
  starting transfers between devices  4.95 us (4%)
  local copies, waits for them, and re-layouts  2.39 us (2%)
    all_gather x1, blocking collectives, local(): got = lax.all_gather(sent, ('grp', 'ep'), axis=0, tiled=True)  32.9 us
    all_gather x1, waiting for transfers between devices, local(): pre = jnp.sum(lax.all_gather(pre, 'grp'), axis=0)  26 us
    all_to_all x1, blocking collectives, local(): lax.all_to_all(blocks, 'rep', split_axis=0, concat_axis=0, tiled=True)  7.14 us
    all_to_all x1, waiting for transfers between devices, local(): lax.all_to_all(out, ('grp', 'ep'), split_axis=0, concat_axis=0, tiled=True)  6.87 us
    all_to_all x1, starting transfers between devices, local(): lax.all_to_all(out, ('grp', 'ep'), split_axis=0, concat_axis=0, tiled=True)  4.87 us
    dot_general x3, matrix products, local(): lax.dot_general(cols[:, i], hidden[:, k * hid:(k + 1) * hid], tn, preferr...  4.31 us
    dot_general x1, matrix products, local(): lax.dot_general(db, w[1], dn, preferred_element_type=f32)  3.24 us
    dot_general x1, matrix products, local(): px = lax.dot_general(da, w[0], dn, preferred_element_type=f32)  3.21 us
  transfers between devices with their start and end apart: 3, of which 2 were waited for; matrix products, arithmetic and copies ran while one was open for 8% of the time, Pallas kernels for 0%

profile of v1, /device:TPU:0, one launch (start us, length us, event | category | flops | bytes accessed | tf_op | source)
XLA Modules:
  0.0 124.9 jit_solution(2781036931998152221)
XLA Ops:
  7.2 0.7 convert_reduce_fusion.2
  8.0 0.1 copy.35
  8.1 0.2 reduce-window.8
  8.4 0.1 fusion.18
  8.5 0.2 convolution_convert_fusion.1
  8.7 1.2 convolution_convert_fusion.2
  10.0 32.9 %all-gather.1 = bf16[8,4,4224]{2,1,0:T(4,128)(2,1)S(1)} all-gather(bf16[1,4,4224]{2,1,0:T(4,128)(2,1)S(1)} %maximum_bitcast_fusion), channel_id=1, replica_groups=mesh['rep'=4,'ep'=4,'grp'=2] {'grp','ep'}, dimensions={0}, use_global_device_ids=true | all-gather | bytes 304128 | tf_op jit(solution)/shard_map/all_gather | solution.py:37
  43.0 0.2 reshape.66
  43.2 0.3 constant_dynamic-slice_fusion
  43.5 2.7 %fusion.2 = f32[32,1792]{1,0:T(8,128)S(1)} fusion(bf16[3,1024,1792]{2,1,0:T(8,128)(2,1)} %bitcast.59, bf16[32,1,1024]{2,1,0:T(2,128)(2,1)S(1)} %get-tuple-element.9), kind=kOutput, calls=%fused_computation.6 | convolution fusion | flops 117440512 | bytes 3964928 | tf_op jit(solution)/shard_map/dot_general | solution.py:49
  46.3 2.7 %fusion.4 = f32[32,1792]{1,0:T(8,128)S(1)} fusion(bf16[3,1024,1792]{2,1,0:T(8,128)(2,1)} %bitcast.60, bf16[32,1,1024]{2,1,0:T(2,128)(2,1)S(1)} %get-tuple-element.9), kind=kOutput, calls=%fused_computation.8 | convolution fusion | flops 117440512 | bytes 3964928 | tf_op jit(solution)/shard_map/dot_general | solution.py:50
  49.0 2.7 %fusion = f32[32,1792]{1,0:T(8,128)S(1)} fusion(bf16[3,1024,1792]{2,1,0:T(8,128)(2,1)} %bitcast.61, bf16[32,1,1024]{2,1,0:T(2,128)(2,1)S(1)} %get-tuple-element.10), kind=kOutput, calls=%fused_computation.2 | convolution fusion | flops 117440512 | bytes 3964928 | tf_op jit(solution)/shard_map/dot_general | solution.py:51
  51.8 0.9 pad_maximum_fusion.1
  52.7 0.2 reshape_reshape.3
  53.0 26.0 %all-gather.7.cloned.1.call-done = f32[64,5376]{1,0:T(8,128)} async-done(((f32[32,5376]{1,0:T(8,128)}), f32[64,5376]{1,0:T(8,128)}) %all-gather.7.cloned.1.call-update) | async-done | bytes 1376272 | tf_op jit(solution)/shard_map/all_gather | solution.py:55
  79.0 1.5 %reduce_sum.66 = f32[32,5376]{1,0:T(8,128)S(1)} reduce(f32[2,32,5376]{2,1,0:T(8,128)} %bitcast.64, f32[]{:T(128)} %constant.10.clone.1), dimensions={0}, to_apply=%region_4.5 | reduce | flops 172032 | bytes 2064388 | tf_op jit(solution)/shard_map/reduce_sum | solution.py:55
  80.5 0.2 multiply_convert_fusion
  80.8 0.8 pad_maximum_fusion.2
  81.5 0.3 constant_dynamic-slice_fusion.1
  81.9 7.1 %all_to_all.14 = bf16[4,32,512]{2,1,0:T(8,128)(2,1)S(1)} all-to-all(bf16[4,32,512]{2,1,0:T(8,128)(2,1)S(1)} %bitcast.66), channel_id=1, replica_groups=mesh['rep'=4,'ep'=4,'grp'=2] {'rep'}, dimensions={0} | all-to-all | bytes 262144 | tf_op jit(solution)/shard_map/all_to_all | solution.py:44
  89.1 3.2 %fusion.1 = f32[32,1024]{1,0:T(8,128)S(1)} fusion(bf16[32,1792]{1,0:T(8,128)(2,1)S(1)} %get-tuple-element.7, bf16[3,1024,1792]{2,1,0:T(8,128)(2,1)} %bitcast.62), kind=kOutput, calls=%fused_computation.5 | convolution fusion | flops 117440512 | bytes 3915776 | tf_op jit(solution)/shard_map/dot_general | solution.py:67
  92.3 3.2 %fusion.6 = bf16[32,1024]{1,0:T(8,128)(2,1)S(1)} fusion(f32[32,1024]{1,0:T(8,128)S(1)} %fusion.1, bf16[32,1792]{1,0:T(8,128)(2,1)S(1)} %get-tuple-element.6, bf16[3,1024,1792]{2,1,0:T(8,128)(2,1)} %bitcast.63), kind=kOutput, calls=%fused_computation.16 | convolution fusion | flops 117506048 | bytes 3981312 | tf_op jit(solution)/shard_map/dot_general | solution.py:68
  95.7 0.7 all_to_all.9
  96.3 4.9 %all-to-all-start = ((bf16[8,4,1152]{2,1,0:T(4,128)(2,1)}), bf16[8,4,1152]{2,1,0:T(4,128)(2,1)S(1)}, u32[]{:S(2)}, u32[]{:S(2)}) async-start(bf16[8,4,1152]{2,1,0:T(4,128)(2,1)} %all_to_all.9), calls=%async_computation | async-start | bytes 147456 | tf_op jit(solution)/shard_map/all_to_all | solution.py:70
  101.2 0.2 fusion.32
  101.4 6.9 %all-to-all-done = bf16[8,4,1152]{2,1,0:T(4,128)(2,1)S(1)} async-done(((bf16[8,4,1152]{2,1,0:T(4,128)(2,1)}), bf16[8,4,1152]{2,1,0:T(4,128)(2,1)S(1)}, u32[]{:S(2)}, u32[]{:S(2)}) %all-to-all-start) | async-done | bytes 73760 | tf_op jit(solution)/shard_map/all_to_all | solution.py:70
  108.5 0.6 broadcast_select_fusion
  109.1 1.8 %convolution_convert_fusion = bf16[128,2048]{1,0:T(8,128)(2,1)} fusion(f32[4,2048]{1,0:T(4,128)S(1)} %bitcast.67, f32[128]{0:T(128)S(1)} %get-tuple-element.3, f32[128]{0:T(128)S(1)} %sub.10), kind=kOutput, calls=%fused_computation.12 | convolution fusion | flops 12846080 | bytes 558080 | tf_op jit(solution)/shard_map/dot_general | solution.py:77
  110.9 1.4 %convolution_bitcast_fusion.1 = f32[256,1,1792]{2,0,1:T(8,128)S(1)} fusion(bf16[128,5376]{1,0:T(8,128)(2,1)} %all-gather.5.cloned.1.call-done, bf16[128,1,256]{2,1,0:T(2,128)(2,1)S(1)} %get-tuple-element.11), kind=kOutput, calls=%fused_computation.10 | convolution fusion | flops 117440512 | bytes 2359296 | tf_op jit(solution)/shard_map/dot_general | solution.py:81
  112.4 1.4 %convolution_bitcast_fusion.2 = f32[256,1,1792]{2,0,1:T(8,128)S(1)} fusion(bf16[128,5376]{1,0:T(8,128)(2,1)} %all-gather.5.cloned.1.call-done, bf16[128,1,256]{2,1,0:T(2,128)(2,1)S(1)} %get-tuple-element.11), kind=kOutput, calls=%fused_computation.11 | convolution fusion | flops 117440512 | bytes 2359296 | tf_op jit(solution)/shard_map/dot_general | solution.py:81
  113.8 1.4 %convolution_bitcast_fusion = f32[256,1,1792]{2,0,1:T(8,128)S(1)} fusion(bf16[128,5376]{1,0:T(8,128)(2,1)} %all-gather.5.cloned.1.call-done, bf16[128,1,256]{2,1,0:T(2,128)(2,1)S(1)} %get-tuple-element.12), kind=kOutput, calls=%fused_computation.9 | convolution fusion | flops 117440512 | bytes 2359296 | tf_op jit(solution)/shard_map/dot_general | solution.py:81
  115.2 2.8 %pad_maximum_fusion = f32[256,3,1792]{2,0,1:T(8,128)} fusion(f32[256,1,1792]{2,0,1:T(8,128)S(1)} %convolution_bitcast_fusion, f32[256,1,1792]{2,0,1:T(8,128)S(1)} %convolution_bitcast_fusion.1, f32[256,1,1792]{2,0,1:T(8,128)S(1)} %convolution_bitcast_fusion.2), kind=kLoop, calls=%fused_computation | loop fusion | flops 2752512 | bytes 11010048 | tf_op jit(solution)/shard_map/stack | solution.py:86
  (25 shorter events, 1.0 us)
Async XLA Ops:
  7.2 1.3 %copy-start = (bf16[128,2048]{1,0:T(8,128)(2,1)S(1)}, bf16[128,2048]{1,0:T(8,128)(2,1)}, u32[]{:S(2)}) copy-start(bf16[128,2048]{1,0:T(8,128)(2,1)} %param.6) | copy-start | bytes 1572868
  7.2 71.8 %all-gather.7.cloned.1.call-start = ((), (), s32[]{:S(2)}) async-start(), calls=%async_computation.3 | async-start | bytes 2064384 | tf_op jit(solution)/shard_map/all_gather | solution.py:55
  52.7 58.2 %all-gather.5.cloned.1.call-start = ((), (), s32[]{:S(2)}) async-start(), calls=%async_computation.2 | async-start | bytes 1720320 | tf_op jit(solution)/shard_map/all_gather | solution.py:65
  89.1 19.4 %copy-start.1 = (s32[128,2]{0,1:T(2,128)S(1)}, s32[128,2]{0,1:T(2,128)}, u32[]{:S(2)}) copy-start(s32[128,2]{0,1:T(2,128)} %param.7) | copy-start | bytes 3076
  96.3 11.9 %all-to-all-start = ((bf16[8,4,1152]{2,1,0:T(4,128)(2,1)}), bf16[8,4,1152]{2,1,0:T(4,128)(2,1)S(1)}, u32[]{:S(2)}, u32[]{:S(2)}) async-start(bf16[8,4,1152]{2,1,0:T(4,128)(2,1)} %all_to_all.9), calls=%async_computation | async-start | bytes 147456 | tf_op jit(solution)/shard_map/all_to_all | solution.py:70
Sparse Core Ops, SparseCore 0:
  52.8 26.1 all-gather.6
  81.7 18.5 all-gather.4
